TPU v7x, 256 devices: a whole 4x4x8 slice. The times are simulated.
256 devices in a mesh: px: 4 (over y_lo, core), py: 8 (over x, y_hi), dom: 8 (over z).
Axes of the slice: x: 4, y: 4 (y_hi: 2, y_lo: 2; y = y_hi * 2 + y_lo), z: 8, core: 2. Of those that a mesh axis runs over, the one named last changes fastest.
Arguments:
- velocity: float32 [16, 64, 256, 128], P('dom', 'px', 'py'), may hold values from 0.65 to 2.2
- buoyancy: float32 [64, 256, 128], P('px', 'py'), may hold values from 0.6 to 1.6
- forward_prev: float32 [16, 64, 256, 128], P('dom', 'px', 'py'), may hold values from -12 to 12
- forward_now: float32 [16, 64, 256, 128], P('dom', 'px', 'py'), may hold values from -12 to 12
- adjoint_prev: float32 [16, 64, 256, 128], P('dom', 'px', 'py'), may hold values from -12 to 12
- adjoint_now: float32 [16, 64, 256, 128], P('dom', 'px', 'py'), may hold values from -12 to 12
- sources: int32 [16], P('dom'), may hold values from 0 to 2097151
- wavelet: float32 [16, 3], P('dom'), may hold values from -800 to 800
- receivers: int32 [16, 1024], P('dom'), may hold values from 0 to 2097151
- misfit: float32 [16, 3, 1024], P('dom'), may hold values from -6 to 6
- sponge: int32 [6], replicated, may hold values from 2 to 8
Outputs:
- forward_before: float32 [16, 64, 256, 128], P('dom', 'px', 'py')
- forward_after: float32 [16, 64, 256, 128], P('dom', 'px', 'py')
- adjoint_before: float32 [16, 64, 256, 128], P('dom', 'px', 'py')
- adjoint_after: float32 [16, 64, 256, 128], P('dom', 'px', 'py')
- drift: float32 [16, 64, 256, 128], P('dom', 'px', 'py')
- spread: float32 [16, 64, 256, 128], P('dom', 'px', 'py')
All inputs are finite; a program needn't handle non-finite values.
Results may differ from a plain program's by a relative error of at most 0.0003.
Values sent between devices are 32-bit elements; how exact they have to be, the bound alone decides.
A program may use at most 64 MiB of HBM per device.

v0:
```python
import jax
import jax.numpy as jnp
from jax import lax
from jax.sharding import PartitionSpec as P

EPSILON = 1e-06
TIME_STEP = 0.18
SPONGE_RATE = 0.5
NEAR_WEIGHT = 9.0 / 8.0
FAR_WEIGHT = 1.0 / 24.0


def with_halo(cells, sides, width):
    for axis, dim in sides:
        count = lax.axis_size(axis)
        ends = count - 1
        head = lax.slice_in_dim(cells, 0, width, axis=dim)
        tail = lax.slice_in_dim(cells, cells.shape[dim] - width, cells.shape[dim], axis=dim)
        cells = jnp.concatenate(
            [
                lax.ppermute(tail, axis, [(i, (i + 1) % count) for i in range(ends)]),
                cells,
                lax.ppermute(head, axis, [((i + 1) % count, i) for i in range(ends)]),
            ],
            axis=dim,
        )
    return cells


def take_slab(source_array, start_at, amount, which_axis):
    return lax.slice_in_dim(
        source_array, start_at, start_at + amount, axis=source_array.ndim + which_axis
    )


def axis_term(wave_field, buoy_field, extent, which_axis):
    half_buoy = 0.5 * (
        take_slab(buoy_field, 1, extent + 3, which_axis)
        + take_slab(buoy_field, 2, extent + 3, which_axis)
    )
    slope_face = NEAR_WEIGHT * (
        take_slab(wave_field, 2, extent + 3, which_axis)
        - take_slab(wave_field, 1, extent + 3, which_axis)
    ) - FAR_WEIGHT * (
        take_slab(wave_field, 3, extent + 3, which_axis)
        - take_slab(wave_field, 0, extent + 3, which_axis)
    )
    flux_face = half_buoy * slope_face
    return NEAR_WEIGHT * (
        take_slab(flux_face, 2, extent, which_axis) - take_slab(flux_face, 1, extent, which_axis)
    ) - FAR_WEIGHT * (
        take_slab(flux_face, 3, extent, which_axis) - take_slab(flux_face, 0, extent, which_axis)
    )


def divergence(padded, buoy_pad):
    size_x = padded.shape[-3] - 6
    size_y = padded.shape[-2] - 6
    size_z = padded.shape[-1] - 6
    along_x = axis_term(
        padded[..., 3 : size_y + 3, 3 : size_z + 3],
        buoy_pad[:, 3 : size_y + 3, 3 : size_z + 3],
        size_x,
        -3,
    )
    along_y = axis_term(
        padded[..., 3 : size_x + 3, :, 3 : size_z + 3],
        buoy_pad[3 : size_x + 3, :, 3 : size_z + 3],
        size_y,
        -2,
    )
    along_z = axis_term(
        padded[..., 3 : size_x + 3, 3 : size_y + 3, :],
        buoy_pad[3 : size_x + 3, 3 : size_y + 3, :],
        size_z,
        -1,
    )
    return along_x + along_y + along_z


def sponge_term(coords, length, low_width, high_width):
    position = coords.astype(jnp.float32)
    far_side = length - 1 - position
    low_float = low_width.astype(jnp.float32)
    high_float = high_width.astype(jnp.float32)
    low_part = jnp.where(
        position < low_float, jnp.square(SPONGE_RATE * (low_float - position) / low_float), 0.0
    )
    high_part = jnp.where(
        far_side < high_float, jnp.square(SPONGE_RATE * (high_float - far_side) / high_float), 0.0
    )
    return low_part + high_part


def plane_tables(flat_index, size_x, size_y, size_z, total_y):
    plane_size = total_y * size_z
    global_x = flat_index // plane_size
    global_y = flat_index // size_z % total_y
    global_z = flat_index % size_z
    local_x = global_x - lax.axis_index("px") * size_x
    local_y = global_y - lax.axis_index("py") * size_y
    inside = (local_x >= 0) & (local_x < size_x) & (local_y >= 0) & (local_y < size_y)
    plane_at = jnp.where(inside, local_x * size_y + local_y, -1)
    plane_hot = (plane_at[..., None] == lax.iota(jnp.int32, size_x * size_y)).astype(jnp.float32)
    depth_hot = (global_z[..., None] == lax.iota(jnp.int32, size_z)).astype(jnp.float32)
    return (plane_hot, depth_hot)


def kernel_from(gram_total, particles):
    diag_part = jnp.diagonal(gram_total)
    dist_sq = diag_part[:, None] + diag_part[None, :] - 2.0 * gram_total
    width = jnp.sum(dist_sq) / (particles * (particles - 1)) + EPSILON
    kernel = jnp.exp(-dist_sq / width)
    return (kernel, jnp.sum(kernel, axis=1))


def on_device(
    velocity,
    buoyancy,
    forward_prev,
    forward_now,
    adjoint_prev,
    adjoint_now,
    sources,
    wavelet,
    receivers,
    misfit,
    sponge,
):
    part_dev, size_x, size_y, size_z = velocity.shape
    block_cells = size_x * size_y * size_z
    total_x = size_x * lax.axis_size("px")
    total_y = size_y * lax.axis_size("py")
    total_cells = total_x * total_y * size_z
    particles = part_dev * lax.axis_size("dom")
    step_sq = TIME_STEP * TIME_STEP
    coords_x = lax.iota(jnp.int32, size_x) + lax.axis_index("px") * size_x
    coords_y = lax.iota(jnp.int32, size_y) + lax.axis_index("py") * size_y
    coords_z = lax.iota(jnp.int32, size_z)
    damping = jnp.exp(
        -(
            sponge_term(coords_x, total_x, sponge[0], sponge[1])[:, None, None]
            + sponge_term(coords_y, total_y, sponge[2], sponge[3])[None, :, None]
            + sponge_term(coords_z, size_z, sponge[4], sponge[5])[None, None, :]
        )
    )
    buoy_rim = with_halo(buoyancy, (("px", 0), ("py", 1)), 3)
    buoy_pad = jnp.pad(buoy_rim, ((0, 0), (0, 0), (3, 3)))
    wave_scale = velocity * velocity / buoyancy
    grad_coef = -2.0 / (velocity * velocity * velocity)
    src_plane, src_depth = plane_tables(sources, size_x, size_y, size_z, total_y)
    src_pattern = (src_plane[:, :, None] * src_depth[:, None, :]).reshape(velocity.shape)
    rec_plane, rec_depth = plane_tables(receivers, size_x, size_y, size_z, total_y)
    previous = jnp.stack([forward_prev, adjoint_prev])
    current = jnp.stack([forward_now, adjoint_now])
    gradient = jnp.zeros_like(velocity)
    for step_at in range(wavelet.shape[1]):
        rimmed = with_halo(current, (("px", 2), ("py", 3)), 3)
        padded = jnp.pad(rimmed, ((0, 0), (0, 0), (0, 0), (0, 0), (3, 3)))
        stepped = 2.0 * current - previous + step_sq * (wave_scale * divergence(padded, buoy_pad))
        weighted_depth = rec_depth * (step_sq * misfit[:, step_at, :])[:, :, None]
        rec_field = jnp.einsum(
            "prq,prz->pqz",
            rec_plane,
            weighted_depth,
            precision=lax.Precision.HIGHEST,
            preferred_element_type=jnp.float32,
        )
        src_field = src_pattern * (step_sq * wavelet[:, step_at])[:, None, None, None]
        injected = jnp.stack(
            [stepped[0] + src_field, stepped[1] + rec_field.reshape(velocity.shape)]
        )
        advanced = damping * injected
        gradient = gradient + grad_coef * current[1] * (
            advanced[0] - 2.0 * current[0] + previous[0]
        )
        previous, current = (current, advanced)
    flat_model = velocity.reshape(part_dev, block_cells)
    flat_grad = gradient.reshape(part_dev, block_cells)
    dom_start = lax.axis_index("dom") * part_dev
    own_sq = lax.psum(jnp.sum(flat_grad * flat_grad, axis=1), ("px", "py"))
    flat_grad = flat_grad / jnp.sqrt(own_sq / total_cells + EPSILON)[:, None]
    model_cols, grad_cols = (
        lax.all_to_all(flat_model, "dom", split_axis=1, concat_axis=0, tiled=True),
        lax.all_to_all(flat_grad, "dom", split_axis=1, concat_axis=0, tiled=True),
    )
    centered = model_cols - jnp.mean(model_cols, axis=0, keepdims=True)
    gram_part = jnp.dot(
        centered, centered.T, precision=lax.Precision.HIGHEST, preferred_element_type=jnp.float32
    )
    gram_total = lax.psum(gram_part, ("px", "py", "dom"))
    kernel, row_sum = kernel_from(gram_total, particles)
    mixed_grad = jnp.dot(
        kernel, grad_cols, precision=lax.Precision.HIGHEST, preferred_element_type=jnp.float32
    )
    mixed_model = jnp.dot(
        kernel, model_cols, precision=lax.Precision.HIGHEST, preferred_element_type=jnp.float32
    )
    drift_flat, model_mix = (
        lax.all_to_all(mixed_grad, "dom", split_axis=0, concat_axis=1, tiled=True),
        lax.all_to_all(mixed_model, "dom", split_axis=0, concat_axis=1, tiled=True),
    )
    own_rowsum = lax.dynamic_slice_in_dim(row_sum, dom_start, part_dev)
    spread_flat = flat_model * own_rowsum[:, None] - model_mix
    return (
        previous[0],
        current[0],
        previous[1],
        current[1],
        drift_flat.reshape(velocity.shape),
        spread_flat.reshape(velocity.shape),
    )


def solution(mesh):
    placed = (
        P("dom", "px", "py", None),
        P("px", "py", None),
        P("dom", "px", "py", None),
        P("dom", "px", "py", None),
        P("dom", "px", "py", None),
        P("dom", "px", "py", None),
        P("dom"),
        P("dom", None),
        P("dom", None),
        P("dom", None, None),
        P(),
    )
    return jax.shard_map(
        on_device,
        mesh=mesh,
        in_specs=placed,
        out_specs=(
            P("dom", "px", "py", None),
            P("dom", "px", "py", None),
            P("dom", "px", "py", None),
            P("dom", "px", "py", None),
            P("dom", "px", "py", None),
            P("dom", "px", "py", None),
        ),
        check_vma=False,
    )
```

profile of v0, /device:TPU:1, one launch (start us, length us, event | category | flops | bytes accessed | tf_op | source)
XLA Modules:
  0.0 337.7 jit_solution(8753166672885361764)
XLA Ops:
  0.7 1.8 fusion.117
  2.5 5.1 %collective-permute-start.3 = (f32[2,2,3,32,128]{4,3,2,1,0:T(8,128)}, f32[2,2,3,32,128]{4,3,2,1,0:T(8,128)S(1)}, u32[]{:S(2)}, u32[]{:S(2)}) collective-permute-start(f32[2,2,3,32,128]{4,3,2,1,0:T(8,128)} %get-tuple-element.33), channel_id=1, source_target_pairs={{64,0},{128,64},{192,128},{65,1},{129,65},{193,129},{66,2},{130,66... | collective-permute-start | bytes 589832 | tf_op jit(solution)/shard_map/ppermute | solution.py:23
  7.6 1.9 collective-permute-start.2
  9.5 1.9 collective-permute-start
  11.5 2.4 collective-permute-start.1
  14.1 1.2 copy.54
  15.3 7.7 %all-to-all-start = ((f32[2,8,8192]{2,0,1:T(2,128)}), f32[2,8,8192]{2,0,1:T(2,128)S(1)}, u32[]{:S(2)}, u32[]{:S(2)}) async-start(f32[2,8,8192]{2,0,1:T(2,128)} %copy.54), calls=%async_computation | async-start | bytes 1048576 | tf_op jit(solution)/shard_map/all_to_all | solution.py:184
  23.4 0.6 fusion.140
  28.1 3.2 fusion.2
  31.4 1.3 collective-permute-start.5
  32.7 5.5 %collective-permute-start.4 = (f32[22,3,128]{2,1,0:T(4,128)S(1)}, f32[22,3,128]{2,1,0:T(4,128)S(1)}, u32[]{:S(2)}, u32[]{:S(2)}) collective-permute-start(f32[22,3,128]{2,1,0:T(4,128)S(1)} %get-tuple-element.36), channel_id=1, source_target_pairs={{0,8},{8,16},{16,24},{24,32},{32,40},{40,48},{48,56},{1,9},{9,17},... | collective-permute-start | bytes 101384 | tf_op jit(solution)/shard_map/ppermute | solution.py:21
  38.2 0.8 fusion.116
  40.2 0.8 pad_maximum_fusion.33
  41.0 1.3 collective-permute-start.7
  42.3 6.9 %collective-permute-start.6 = (f32[2,2,22,3,128]{4,3,2,1,0:T(4,128)}, f32[2,2,22,3,128]{4,3,2,1,0:T(4,128)}, u32[]{:S(2)}, u32[]{:S(2)}) collective-permute-start(f32[2,2,22,3,128]{4,3,2,1,0:T(4,128)} %get-tuple-element.20), channel_id=1, source_target_pairs={{0,8},{8,16},{16,24},{24,32},{32,40},{40,48},{48,56},{1,9},{9,17},... | collective-permute-start | bytes 405512 | tf_op jit(solution)/shard_map/ppermute | solution.py:21
  49.2 1.2 pad_maximum_fusion.4
  51.1 1.0 broadcast_subtract_fusion
  52.1 1.4 sub.399
  53.5 0.8 fusion.141
  54.3 79.6 %psum.14 = f32[16,16]{1,0:T(8,128)S(1)} all-reduce(f32[16,16]{1,0:T(8,128)S(1)} %fusion.141), channel_id=1, replica_groups=mesh['px'=4,'py'=8,'dom'=8] {'px','py','dom'}, use_global_device_ids=true, to_apply=%region_1.2 | all-reduce | flops 256 | bytes 2048 | tf_op jit(solution)/shard_map/psum | solution.py:191
  133.9 0.7 gather_fusion
  134.6 0.7 fusion.125
  136.1 0.6 fusion.121
  136.7 1.2 copy.60
  137.9 5.5 %all-to-all-start.3 = ((f32[8,2,8192]{2,1,0:T(2,128)}), f32[8,2,8192]{2,1,0:T(2,128)}, u32[]{:S(2)}, u32[]{:S(2)}) async-start(f32[8,2,8192]{2,1,0:T(2,128)} %copy.60), calls=%async_computation.3 | async-start | bytes 1048576 | tf_op jit(solution)/shard_map/all_to_all | solution.py:201
  143.3 2.4 fusion.47
  145.8 1.3 pad_maximum_fusion
  147.1 3.1 fusion.6
  150.2 2.6 fusion.37
  152.8 8.6 %all-to-all-done.3 = f32[8,2,8192]{2,1,0:T(2,128)} async-done(((f32[8,2,8192]{2,1,0:T(2,128)}), f32[8,2,8192]{2,1,0:T(2,128)}, u32[]{:S(2)}, u32[]{:S(2)}) %all-to-all-start.3) | async-done | bytes 524320 | tf_op jit(solution)/shard_map/all_to_all | solution.py:201
  161.4 2.1 copy.61
  163.5 1.9 all_to_all.59
  165.5 2.4 multiply_subtract_fusion
  167.8 4.3 %fusion.84 = f32[2,2,16,32,128]{4,3,2,1,0:T(8,128)S(1)} fusion(f32[2,2,16,32,131]{4,3,2,1,0:T(8,128)} %fusion.6, f32[2,2,16,35,128]{4,3,2,1,0:T(8,128)S(1)} %copy-done.2, f32[2,2,19,32,128]{4,3,2,1,0:T(8,128)S(1)} %fusion.47, f32[1,2,16,32,128]{4,3,2,1,0:T(8,128)S(1)} %bitcast.82, f32[1,2,16,32,128]{4,3,2,1,0:T(8,128)S(1)} %bitcast.81, ...), kind=kLoop, calls=%fused_computation.153 | loop fusion | flops 6291456 | bytes 16252928 | tf_op jit(solution)/shard_map/add | solution.py:160
  172.6 2.4 collective-permute-start.9
  175.0 3.2 collective-permute-start.8
  178.2 2.5 fusion.1
  180.8 1.3 collective-permute-start.11
  182.1 5.6 %collective-permute-start.10 = (f32[2,2,22,3,128]{4,3,2,1,0:T(4,128)S(1)}, f32[2,2,22,3,128]{4,3,2,1,0:T(4,128)S(1)}, u32[]{:S(2)}, u32[]{:S(2)}) collective-permute-start(f32[2,2,22,3,128]{4,3,2,1,0:T(4,128)S(1)} %get-tuple-element.18), channel_id=1, source_target_pairs={{0,8},{8,16},{16,24},{24,32},{32,40},{40,48},{48,56},{1,9},{9,17},... | collective-permute-start | bytes 405512 | tf_op jit(solution)/shard_map/ppermute | solution.py:21
  188.3 1.9 collective-permute-done.11
  190.2 2.4 collective-permute-done.10
  192.9 1.7 fusion.12
  194.6 0.6 fusion.32
  195.2 1.3 fusion.70
  196.9 2.3 collective-permute-start.13
  199.2 3.5 %collective-permute-start.12 = (f32[2,2,3,32,128]{4,3,2,1,0:T(8,128)S(1)}, f32[2,2,3,32,128]{4,3,2,1,0:T(8,128)S(1)}, u32[]{:S(2)}, u32[]{:S(2)}) collective-permute-start(f32[2,2,3,32,128]{4,3,2,1,0:T(8,128)S(1)} %get-tuple-element.24), channel_id=1, source_target_pairs={{0,64},{64,128},{128,192},{1,65},{65,129},{129,193},{2,66},{66,130... | collective-permute-start | bytes 589832 | tf_op jit(solution)/shard_map/ppermute | solution.py:21
  202.7 2.5 fusion
  205.3 1.3 collective-permute-start.15
  206.6 6.3 %collective-permute-start.14 = (f32[2,2,22,3,128]{4,3,2,1,0:T(4,128)S(1)}, f32[2,2,22,3,128]{4,3,2,1,0:T(4,128)S(1)}, u32[]{:S(2)}, u32[]{:S(2)}) collective-permute-start(f32[2,2,22,3,128]{4,3,2,1,0:T(4,128)S(1)} %get-tuple-element.16), channel_id=1, source_target_pairs={{0,8},{8,16},{16,24},{24,32},{32,40},{40,48},{48,56},{1,9},{9,17},... | collective-permute-start | bytes 405512 | tf_op jit(solution)/shard_map/ppermute | solution.py:21
  213.4 1.6 collective-permute-done.15
  215.1 4.6 %collective-permute-done.14 = f32[2,2,22,3,128]{4,3,2,1,0:T(4,128)S(1)} collective-permute-done((f32[2,2,22,3,128]{4,3,2,1,0:T(4,128)S(1)}, f32[2,2,22,3,128]{4,3,2,1,0:T(4,128)S(1)}, u32[]{:S(2)}, u32[]{:S(2)}) %collective-permute-start.14) | collective-permute-done | bytes 135200 | tf_op jit(solution)/shard_map/ppermute | solution.py:21
  220.0 1.7 fusion.18
  221.7 0.6 fusion.27
  222.3 1.3 fusion.56
  223.9 0.9 copy-done.9
  224.8 1.6 multiply_reduce_fusion
  226.5 68.9 %psum.15 = f32[2]{0:T(128)S(1)} all-reduce(f32[2]{0:T(128)S(1)} %get-tuple-element.11), channel_id=1, replica_groups=mesh['px'=4,'py'=8,'dom'=8] {'px','py'}, use_global_device_ids=true, to_apply=%region_4.5 | all-reduce | flops 2 | bytes 16 | tf_op jit(solution)/shard_map/psum | solution.py:181
  295.9 19.1 %all_to_all.64 = f32[2,8,8192]{2,0,1:T(2,128)S(1)} all-to-all(f32[2,8,8192]{2,0,1:T(2,128)S(1)} %copy.55), channel_id=1, replica_groups=mesh['px'=4,'py'=8,'dom'=8] {'dom'}, dimensions={1} | all-to-all | bytes 1048576 | tf_op jit(solution)/shard_map/all_to_all | solution.py:185
  315.4 0.6 fusion.123
  315.9 1.2 copy.57
  317.1 3.5 %all-to-all-start.2 = ((f32[8,2,8192]{2,1,0:T(2,128)}), f32[8,2,8192]{2,1,0:T(2,128)S(1)}, u32[]{:S(2)}, u32[]{:S(2)}) async-start(f32[8,2,8192]{2,1,0:T(2,128)} %copy.57), calls=%async_computation.2 | async-start | bytes 1048576 | tf_op jit(solution)/shard_map/all_to_all | solution.py:200
  320.6 0.8 slice_bitcast_fusion.2
  321.5 15.1 %all-to-all-done.2 = f32[8,2,8192]{2,1,0:T(2,128)S(1)} async-done(((f32[8,2,8192]{2,1,0:T(2,128)}), f32[8,2,8192]{2,1,0:T(2,128)S(1)}, u32[]{:S(2)}, u32[]{:S(2)}) %all-to-all-start.2) | async-done | bytes 524320 | tf_op jit(solution)/shard_map/all_to_all | solution.py:200
  336.9 0.9 reshape.285
  (99 shorter events, 7.3 us)
Async XLA Ops:
  0.6 8.9 %copy-start.11 = (f32[16,32,128]{2,1,0:T(8,128)S(1)}, f32[16,32,128]{2,1,0:T(8,128)}, u32[]{:S(2)}) copy-start(f32[16,32,128]{2,1,0:T(8,128)} %param.12) | copy-start | bytes 786436
  0.6 13.2 %copy-start.8 = (f32[2,16,32,128]{3,2,1,0:T(8,128)S(1)}, f32[2,16,32,128]{3,2,1,0:T(8,128)}, u32[]{:S(2)}) copy-start(f32[2,16,32,128]{3,2,1,0:T(8,128)} %param.11) | copy-start | bytes 1572868
  2.5 37.4 %collective-permute-start.3 = (f32[2,2,3,32,128]{4,3,2,1,0:T(8,128)}, f32[2,2,3,32,128]{4,3,2,1,0:T(8,128)S(1)}, u32[]{:S(2)}, u32[]{:S(2)}) collective-permute-start(f32[2,2,3,32,128]{4,3,2,1,0:T(8,128)} %get-tuple-element.33), channel_id=1, source_target_pairs={{64,0},{128,64},{192,128},{65,1},{129,65},{193,129},{66,2},{130,66... | collective-permute-start | bytes 589832 | tf_op jit(solution)/shard_map/ppermute | solution.py:23
  7.6 32.3 %collective-permute-start.2 = (f32[2,2,3,32,128]{4,3,2,1,0:T(8,128)S(1)}, f32[2,2,3,32,128]{4,3,2,1,0:T(8,128)S(1)}, u32[]{:S(2)}, u32[]{:S(2)}) collective-permute-start(f32[2,2,3,32,128]{4,3,2,1,0:T(8,128)S(1)} %get-tuple-element.32), channel_id=1, source_target_pairs={{0,64},{64,128},{128,192},{1,65},{65,129},{129,193},{2,66},{66,130... | collective-permute-start | bytes 589832 | tf_op jit(solution)/shard_map/ppermute | solution.py:21
  9.5 21.8 %collective-permute-start = (f32[3,32,128]{2,1,0:T(8,128)S(1)}, f32[3,32,128]{2,1,0:T(8,128)S(1)}, u32[]{:S(2)}, u32[]{:S(2)}) collective-permute-start(f32[3,32,128]{2,1,0:T(8,128)S(1)} %get-tuple-element.39), channel_id=1, source_target_pairs={{0,64},{64,128},{128,192},{1,65},{65,129},{129,193},{2,66},{66,130... | collective-permute-start | bytes 147464 | tf_op jit(solution)/shard_map/ppermute | solution.py:21
  11.5 19.9 %collective-permute-start.1 = (f32[3,32,128]{2,1,0:T(8,128)S(1)}, f32[3,32,128]{2,1,0:T(8,128)S(1)}, u32[]{:S(2)}, u32[]{:S(2)}) collective-permute-start(f32[3,32,128]{2,1,0:T(8,128)S(1)} %get-tuple-element.38), channel_id=1, source_target_pairs={{64,0},{128,64},{192,128},{65,1},{129,65},{193,129},{66,2},{130,66... | collective-permute-start | bytes 147464 | tf_op jit(solution)/shard_map/ppermute | solution.py:23
  14.0 8.9 %copy-start.16 = (f32[2,3]{1,0:T(2,128)S(1)}, f32[2,3]{1,0:T(2,128)}, u32[]{:S(2)}) copy-start(f32[2,3]{1,0:T(2,128)} %param.18) | copy-start | bytes 76
  14.0 9.2 %copy-start.18 = (s32[2]{0:T(128)S(1)}, s32[2]{0:T(128)}, u32[]{:S(2)}) copy-start(s32[2]{0:T(128)} %param.17) | copy-start | bytes 28
  14.0 9.3 %copy-start.17 = (s32[2,1024]{1,0:T(2,128)S(1)}, s32[2,1024]{1,0:T(2,128)}, u32[]{:S(2)}) copy-start(s32[2,1024]{1,0:T(2,128)} %param.19) | copy-start | bytes 24580
  14.0 9.3 %copy-start.14 = (f32[2,3,1024]{2,0,1:T(2,128)S(1)}, f32[2,3,1024]{2,0,1:T(2,128)}, u32[]{:S(2)}) copy-start(f32[2,3,1024]{2,0,1:T(2,128)} %param.20) | copy-start | bytes 73732
  14.0 9.3 %copy-start.15 = (s32[6]{0:T(128)S(1)}, s32[6]{0:T(128)}, u32[]{:S(2)}) copy-start(s32[6]{0:T(128)} %param.21) | copy-start | bytes 76
  15.3 35.2 %all-to-all-start = ((f32[2,8,8192]{2,0,1:T(2,128)}), f32[2,8,8192]{2,0,1:T(2,128)S(1)}, u32[]{:S(2)}, u32[]{:S(2)}) async-start(f32[2,8,8192]{2,0,1:T(2,128)} %copy.54), calls=%async_computation | async-start | bytes 1048576 | tf_op jit(solution)/shard_map/all_to_all | solution.py:184
  31.4 7.6 %collective-permute-start.5 = (f32[22,3,128]{2,1,0:T(4,128)S(1)}, f32[22,3,128]{2,1,0:T(4,128)S(1)}, u32[]{:S(2)}, u32[]{:S(2)}) collective-permute-start(f32[22,3,128]{2,1,0:T(4,128)S(1)} %get-tuple-element.37), channel_id=1, source_target_pairs={{8,0},{16,8},{24,16},{32,24},{40,32},{48,40},{56,48},{9,1},{17,9},... | collective-permute-start | bytes 101384 | tf_op jit(solution)/shard_map/ppermute | solution.py:23
  32.7 6.6 %collective-permute-start.4 = (f32[22,3,128]{2,1,0:T(4,128)S(1)}, f32[22,3,128]{2,1,0:T(4,128)S(1)}, u32[]{:S(2)}, u32[]{:S(2)}) collective-permute-start(f32[22,3,128]{2,1,0:T(4,128)S(1)} %get-tuple-element.36), channel_id=1, source_target_pairs={{0,8},{8,16},{16,24},{24,32},{32,40},{40,48},{48,56},{1,9},{9,17},... | collective-permute-start | bytes 101384 | tf_op jit(solution)/shard_map/ppermute | solution.py:21
  39.0 1.0 copy-start
  39.0 1.2 copy-start.1
  39.9 10.6 %copy-start.4 = (f32[2,2,3,32,128]{4,3,2,1,0:T(8,128)}, f32[2,2,3,32,128]{4,3,2,1,0:T(8,128)S(1)}, u32[]{:S(2)}) copy-start(f32[2,2,3,32,128]{4,3,2,1,0:T(8,128)S(1)} %collective-permute-done.3) | copy-start | bytes 589828
  40.2 10.3 %copy-start.6 = (f32[2,2,3,32,128]{4,3,2,1,0:T(8,128)}, f32[2,2,3,32,128]{4,3,2,1,0:T(8,128)S(1)}, u32[]{:S(2)}) copy-start(f32[2,2,3,32,128]{4,3,2,1,0:T(8,128)S(1)} %collective-permute-done.2) | copy-start | bytes 589828
  41.0 104.7 %collective-permute-start.7 = (f32[2,2,22,3,128]{4,3,2,1,0:T(4,128)}, f32[2,2,22,3,128]{4,3,2,1,0:T(4,128)}, u32[]{:S(2)}, u32[]{:S(2)}) collective-permute-start(f32[2,2,22,3,128]{4,3,2,1,0:T(4,128)} %get-tuple-element.21), channel_id=1, source_target_pairs={{8,0},{16,8},{24,16},{32,24},{40,32},{48,40},{56,48},{9,1},{17,9},... | collective-permute-start | bytes 405512 | tf_op jit(solution)/shard_map/ppermute | solution.py:23
  42.3 103.5 %collective-permute-start.6 = (f32[2,2,22,3,128]{4,3,2,1,0:T(4,128)}, f32[2,2,22,3,128]{4,3,2,1,0:T(4,128)}, u32[]{:S(2)}, u32[]{:S(2)}) collective-permute-start(f32[2,2,22,3,128]{4,3,2,1,0:T(4,128)} %get-tuple-element.20), channel_id=1, source_target_pairs={{0,8},{8,16},{16,24},{24,32},{32,40},{40,48},{48,56},{1,9},{9,17},... | collective-permute-start | bytes 405512 | tf_op jit(solution)/shard_map/ppermute | solution.py:21
  137.9 23.5 %all-to-all-start.3 = ((f32[8,2,8192]{2,1,0:T(2,128)}), f32[8,2,8192]{2,1,0:T(2,128)}, u32[]{:S(2)}, u32[]{:S(2)}) async-start(f32[8,2,8192]{2,1,0:T(2,128)} %copy.60), calls=%async_computation.3 | async-start | bytes 1048576 | tf_op jit(solution)/shard_map/all_to_all | solution.py:201
  143.3 2.5 copy-start.5
  143.3 2.5 copy-start.7
  165.4 2.4 copy-start.2
  165.4 2.4 copy-start.10
  165.5 2.4 copy-start.12
  167.8 4.3 %copy-start.13 = (f32[2,512,128]{2,1,0:T(8,128)S(1)}, f32[2,512,128]{2,1,0:T(8,128)}, u32[]{:S(2)}) copy-start(f32[2,512,128]{2,1,0:T(8,128)} %fusion.2) | copy-start | bytes 1572868
  172.6 8.1 %collective-permute-start.9 = (f32[2,2,3,32,128]{4,3,2,1,0:T(8,128)S(1)}, f32[2,2,3,32,128]{4,3,2,1,0:T(8,128)S(1)}, u32[]{:S(2)}, u32[]{:S(2)}) collective-permute-start(f32[2,2,3,32,128]{4,3,2,1,0:T(8,128)S(1)} %get-tuple-element.29), channel_id=1, source_target_pairs={{64,0},{128,64},{192,128},{65,1},{129,65},{193,129},{66,2},{130,66... | collective-permute-start | bytes 589832 | tf_op jit(solution)/shard_map/ppermute | solution.py:23
  175.0 5.8 %collective-permute-start.8 = (f32[2,2,3,32,128]{4,3,2,1,0:T(8,128)S(1)}, f32[2,2,3,32,128]{4,3,2,1,0:T(8,128)S(1)}, u32[]{:S(2)}, u32[]{:S(2)}) collective-permute-start(f32[2,2,3,32,128]{4,3,2,1,0:T(8,128)S(1)} %get-tuple-element.28), channel_id=1, source_target_pairs={{0,64},{64,128},{128,192},{1,65},{65,129},{129,193},{2,66},{66,130... | collective-permute-start | bytes 589832 | tf_op jit(solution)/shard_map/ppermute | solution.py:21
  180.8 9.3 %collective-permute-start.11 = (f32[2,2,22,3,128]{4,3,2,1,0:T(4,128)S(1)}, f32[2,2,22,3,128]{4,3,2,1,0:T(4,128)S(1)}, u32[]{:S(2)}, u32[]{:S(2)}) collective-permute-start(f32[2,2,22,3,128]{4,3,2,1,0:T(4,128)S(1)} %get-tuple-element.19), channel_id=1, source_target_pairs={{8,0},{16,8},{24,16},{32,24},{40,32},{48,40},{56,48},{9,1},{17,9},... | collective-permute-start | bytes 405512 | tf_op jit(solution)/shard_map/ppermute | solution.py:23
  182.1 5.8 %copy-start.3 = (f32[19,32,128]{2,1,0:T(8,128)S(1)}, f32[19,32,128]{2,1,0:T(8,128)}, u32[]{:S(2)}) copy-start(f32[19,32,128]{2,1,0:T(8,128)} %fusion.116) | copy-start | bytes 933892
  182.1 10.5 %collective-permute-start.10 = (f32[2,2,22,3,128]{4,3,2,1,0:T(4,128)S(1)}, f32[2,2,22,3,128]{4,3,2,1,0:T(4,128)S(1)}, u32[]{:S(2)}, u32[]{:S(2)}) collective-permute-start(f32[2,2,22,3,128]{4,3,2,1,0:T(4,128)S(1)} %get-tuple-element.18), channel_id=1, source_target_pairs={{0,8},{8,16},{16,24},{24,32},{32,40},{40,48},{48,56},{1,9},{9,17},... | collective-permute-start | bytes 405512 | tf_op jit(solution)/shard_map/ppermute | solution.py:21
  196.9 8.3 %collective-permute-start.13 = (f32[2,2,3,32,128]{4,3,2,1,0:T(8,128)S(1)}, f32[2,2,3,32,128]{4,3,2,1,0:T(8,128)S(1)}, u32[]{:S(2)}, u32[]{:S(2)}) collective-permute-start(f32[2,2,3,32,128]{4,3,2,1,0:T(8,128)S(1)} %get-tuple-element.25), channel_id=1, source_target_pairs={{64,0},{128,64},{192,128},{65,1},{129,65},{193,129},{66,2},{130,66... | collective-permute-start | bytes 589832 | tf_op jit(solution)/shard_map/ppermute | solution.py:23
  199.2 6.0 %collective-permute-start.12 = (f32[2,2,3,32,128]{4,3,2,1,0:T(8,128)S(1)}, f32[2,2,3,32,128]{4,3,2,1,0:T(8,128)S(1)}, u32[]{:S(2)}, u32[]{:S(2)}) collective-permute-start(f32[2,2,3,32,128]{4,3,2,1,0:T(8,128)S(1)} %get-tuple-element.24), channel_id=1, source_target_pairs={{0,64},{64,128},{128,192},{1,65},{65,129},{129,193},{2,66},{66,130... | collective-permute-start | bytes 589832 | tf_op jit(solution)/shard_map/ppermute | solution.py:21
  205.3 9.8 %collective-permute-start.15 = (f32[2,2,22,3,128]{4,3,2,1,0:T(4,128)S(1)}, f32[2,2,22,3,128]{4,3,2,1,0:T(4,128)S(1)}, u32[]{:S(2)}, u32[]{:S(2)}) collective-permute-start(f32[2,2,22,3,128]{4,3,2,1,0:T(4,128)S(1)} %get-tuple-element.17), channel_id=1, source_target_pairs={{8,0},{16,8},{24,16},{32,24},{40,32},{48,40},{56,48},{9,1},{17,9},... | collective-permute-start | bytes 405512 | tf_op jit(solution)/shard_map/ppermute | solution.py:23
  206.6 13.1 %collective-permute-start.14 = (f32[2,2,22,3,128]{4,3,2,1,0:T(4,128)S(1)}, f32[2,2,22,3,128]{4,3,2,1,0:T(4,128)S(1)}, u32[]{:S(2)}, u32[]{:S(2)}) collective-permute-start(f32[2,2,22,3,128]{4,3,2,1,0:T(4,128)S(1)} %get-tuple-element.16), channel_id=1, source_target_pairs={{0,8},{8,16},{16,24},{24,32},{32,40},{40,48},{48,56},{1,9},{9,17},... | collective-permute-start | bytes 405512 | tf_op jit(solution)/shard_map/ppermute | solution.py:21
  223.8 1.0 copy-start.9
  317.1 19.4 %all-to-all-start.2 = ((f32[8,2,8192]{2,1,0:T(2,128)}), f32[8,2,8192]{2,1,0:T(2,128)S(1)}, u32[]{:S(2)}, u32[]{:S(2)}) async-start(f32[8,2,8192]{2,1,0:T(2,128)} %copy.57), calls=%async_computation.2 | async-start | bytes 1048576 | tf_op jit(solution)/shard_map/all_to_all | solution.py:200
where the time goes:
time: 339 us; the launch traced here: 338 us
  blocking collectives  168 us (50%)
  starting transfers between devices  68.8 us (20%)
  other arithmetic  35.5 us (10%)
  waiting for transfers between devices  34.7 us (10%)
  local copies, waits for them, and re-layouts  15.2 us (4%)
  matrix products  10.2 us (3%)
  between operations  5.78 us (2%)
    psum x1, blocking collectives, on_device(): gram_total = lax.psum(gram_part, ('px', 'py', 'dom'))  79.6 us
    psum x1, blocking collectives, on_device(): own_sq = lax.psum(jnp.sum(flat_grad * flat_grad, axis=1), ('px', 'py'))  68.9 us
    ppermute x8, starting transfers between devices, with_halo(): lax.ppermute(tail, axis, [(i, (i + 1) % count) for i in range(ends)])  34.8 us
    all_to_all x1, blocking collectives, on_device(): lax.all_to_all(flat_grad, 'dom', split_axis=1, concat_axis=0, tiled=True)  19.1 us
    ppermute x8, starting transfers between devices, with_halo(): lax.ppermute(head, axis, [((i + 1) % count, i) for i in range(ends)])  17.4 us
    all_to_all x1, waiting for transfers between devices, on_device(): lax.all_to_all(mixed_grad, 'dom', split_axis=0, concat_axis=1, tiled=True)  15.1 us
    mul x9, other arithmetic, axis_term(): flux_face = half_buoy * slope_face  13.4 us
    all_to_all x1, waiting for transfers between devices, on_device(): lax.all_to_all(mixed_model, 'dom', split_axis=0, concat_axis=1, tiled=True)  8.58 us
  transfers between devices with their start and end apart: 19, of which 8 were waited for; matrix products, arithmetic and copies ran while one was open for 10% of the time, Pallas kernels for 0%

commit v1 on v0

--- a/solution.py
+++ b/solution.py
@@ -178,7 +178,9 @@
     flat_model = velocity.reshape(part_dev, block_cells)
     flat_grad = gradient.reshape(part_dev, block_cells)
     dom_start = lax.axis_index("dom") * part_dev
-    own_sq = lax.psum(jnp.sum(flat_grad * flat_grad, axis=1), ("px", "py"))
+    own_sq = jnp.sum(flat_grad * flat_grad, axis=1)
+    for mesh_axis in ("py", "px"):
+        own_sq = lax.psum(own_sq, mesh_axis)
     flat_grad = flat_grad / jnp.sqrt(own_sq / total_cells + EPSILON)[:, None]
     model_cols, grad_cols = (
         lax.all_to_all(flat_model, "dom", split_axis=1, concat_axis=0, tiled=True),

time: 339 us -> 299 us (0.88)
  blocking collectives: 168 us -> 127 us
    psum x1 -> x2, blocking collectives: 68.9 us -> 28.3 us  [on_device(): own_sq = lax.psum(own_sq, mesh_axis)]
  transfers between devices with their start and end apart: 19 -> 19, of which waited for: 8 -> 8; matrix products, arithmetic and copies ran while one was open for 10% -> 11% of each run, Pallas kernels for 0% -> 0%
where the time goes in v1:
time: 299 us; the launch traced here: 297 us
  blocking collectives  127 us (42%)
  starting transfers between devices  68.8 us (23%)
  other arithmetic  35.5 us (12%)
  waiting for transfers between devices  34.7 us (12%)
  local copies, waits for them, and re-layouts  15.2 us (5%)
  matrix products  10.2 us (3%)
  between operations  5.87 us (2%)
    psum x1, blocking collectives, on_device(): gram_total = lax.psum(gram_part, ('px', 'py', 'dom'))  79.6 us
    ppermute x8, starting transfers between devices, with_halo(): lax.ppermute(tail, axis, [(i, (i + 1) % count) for i in range(ends)])  34.8 us
    psum x2, blocking collectives, on_device(): own_sq = lax.psum(own_sq, mesh_axis)  28.3 us
    all_to_all x1, blocking collectives, on_device(): lax.all_to_all(flat_grad, 'dom', split_axis=1, concat_axis=0, tiled=True)  19.2 us
    ppermute x8, starting transfers between devices, with_halo(): lax.ppermute(head, axis, [((i + 1) % count, i) for i in range(ends)])  17.4 us
    all_to_all x1, waiting for transfers between devices, on_device(): lax.all_to_all(mixed_grad, 'dom', split_axis=0, concat_axis=1, tiled=True)  15.1 us
    mul x9, other arithmetic, axis_term(): flux_face = half_buoy * slope_face  13.4 us
    all_to_all x1, waiting for transfers between devices, on_device(): lax.all_to_all(mixed_model, 'dom', split_axis=0, concat_axis=1, tiled=True)  8.59 us
  transfers between devices with their start and end apart: 19, of which 8 were waited for; matrix products, arithmetic and copies ran while one was open for 11% of the time, Pallas kernels for 0%

profile of v1, /device:TPU:1, one launch (start us, length us, event | category | flops | bytes accessed | tf_op | source)
XLA Modules:
  0.0 297.4 jit_solution(2518572764122210080)
XLA Ops:
  0.7 1.8 fusion.117
  2.5 5.1 %collective-permute-start.3 = (f32[2,2,3,32,128]{4,3,2,1,0:T(8,128)}, f32[2,2,3,32,128]{4,3,2,1,0:T(8,128)S(1)}, u32[]{:S(2)}, u32[]{:S(2)}) collective-permute-start(f32[2,2,3,32,128]{4,3,2,1,0:T(8,128)} %get-tuple-element.33), channel_id=1, source_target_pairs={{64,0},{128,64},{192,128},{65,1},{129,65},{193,129},{66,2},{130,66... | collective-permute-start | bytes 589832 | tf_op jit(solution)/shard_map/ppermute | solution.py:23
  7.6 1.9 collective-permute-start.2
  9.5 1.9 collective-permute-start
  11.5 2.4 collective-permute-start.1
  14.1 1.2 copy.54
  15.3 7.7 %all-to-all-start = ((f32[2,8,8192]{2,0,1:T(2,128)}), f32[2,8,8192]{2,0,1:T(2,128)S(1)}, u32[]{:S(2)}, u32[]{:S(2)}) async-start(f32[2,8,8192]{2,0,1:T(2,128)} %copy.54), calls=%async_computation | async-start | bytes 1048576 | tf_op jit(solution)/shard_map/all_to_all | solution.py:186
  23.4 0.7 fusion.140
  28.3 3.2 %fusion.2 = f32[2,512,128]{2,1,0:T(8,128)} fusion(s32[2,1024]{1,0:T(2,128)S(1)} %get-tuple-element.44, f32[2,1024]{1,0:T(2,128)S(1)} %get-tuple-element.41, s32[2,1024]{1,0:T(2,128)S(1)} %get-tuple-element.43), kind=kOutput, calls=%fused_computation.16 | convolution fusion | flops 1612185600 | bytes 548864 | tf_op jit(solution)/shard_map/prq,prz->pqz/dot_general | solution.py:162
  31.6 1.3 collective-permute-start.5
  32.9 5.5 %collective-permute-start.4 = (f32[22,3,128]{2,1,0:T(4,128)S(1)}, f32[22,3,128]{2,1,0:T(4,128)S(1)}, u32[]{:S(2)}, u32[]{:S(2)}) collective-permute-start(f32[22,3,128]{2,1,0:T(4,128)S(1)} %get-tuple-element.36), channel_id=1, source_target_pairs={{0,8},{8,16},{16,24},{24,32},{32,40},{40,48},{48,56},{1,9},{9,17},... | collective-permute-start | bytes 101384 | tf_op jit(solution)/shard_map/ppermute | solution.py:21
  38.4 0.8 fusion.116
  40.3 0.8 pad_maximum_fusion.33
  41.2 1.3 collective-permute-start.7
  42.5 6.9 %collective-permute-start.6 = (f32[2,2,22,3,128]{4,3,2,1,0:T(4,128)}, f32[2,2,22,3,128]{4,3,2,1,0:T(4,128)}, u32[]{:S(2)}, u32[]{:S(2)}) collective-permute-start(f32[2,2,22,3,128]{4,3,2,1,0:T(4,128)} %get-tuple-element.20), channel_id=1, source_target_pairs={{0,8},{8,16},{16,24},{24,32},{32,40},{40,48},{48,56},{1,9},{9,17},... | collective-permute-start | bytes 405512 | tf_op jit(solution)/shard_map/ppermute | solution.py:21
  49.4 1.2 pad_maximum_fusion.4
  51.2 1.0 broadcast_subtract_fusion
  52.2 1.4 sub.399
  53.6 0.8 fusion.141
  54.4 79.6 %psum.21 = f32[16,16]{1,0:T(8,128)S(1)} all-reduce(f32[16,16]{1,0:T(8,128)S(1)} %fusion.141), channel_id=1, replica_groups=mesh['px'=4,'py'=8,'dom'=8] {'px','py','dom'}, use_global_device_ids=true, to_apply=%region_1.2 | all-reduce | flops 256 | bytes 2048 | tf_op jit(solution)/shard_map/psum | solution.py:193
  134.0 0.7 gather_fusion
  134.7 0.7 fusion.125
  136.2 0.6 fusion.121
  136.8 1.2 copy.60
  138.0 5.5 %all-to-all-start.3 = ((f32[8,2,8192]{2,1,0:T(2,128)}), f32[8,2,8192]{2,1,0:T(2,128)}, u32[]{:S(2)}, u32[]{:S(2)}) async-start(f32[8,2,8192]{2,1,0:T(2,128)} %copy.60), calls=%async_computation.3 | async-start | bytes 1048576 | tf_op jit(solution)/shard_map/all_to_all | solution.py:203
  143.5 2.4 fusion.47
  145.9 1.3 pad_maximum_fusion
  147.2 3.1 %fusion.6 = f32[2,2,16,32,131]{4,3,2,1,0:T(8,128)} fusion(f32[2,2,22,38,128]{4,3,2,1,0:T(8,128)S(1)} %pad_maximum_fusion, f32[16,32,131]{2,1,0:T(8,128)S(1)} %fusion.101), kind=kLoop, calls=%fused_computation.20 | loop fusion | flops 1609728 | bytes 3053568 | tf_op jit(solution)/shard_map/mul | solution.py:48
  150.3 2.6 fusion.37
  152.9 8.6 %all-to-all-done.3 = f32[8,2,8192]{2,1,0:T(2,128)} async-done(((f32[8,2,8192]{2,1,0:T(2,128)}), f32[8,2,8192]{2,1,0:T(2,128)}, u32[]{:S(2)}, u32[]{:S(2)}) %all-to-all-start.3) | async-done | bytes 524320 | tf_op jit(solution)/shard_map/all_to_all | solution.py:203
  161.5 2.1 copy.61
  163.7 1.9 all_to_all.59
  165.6 2.4 multiply_subtract_fusion
  168.0 4.3 %fusion.84 = f32[2,2,16,32,128]{4,3,2,1,0:T(8,128)S(1)} fusion(f32[2,2,16,32,131]{4,3,2,1,0:T(8,128)} %fusion.6, f32[2,2,16,35,128]{4,3,2,1,0:T(8,128)S(1)} %copy-done.2, f32[2,2,19,32,128]{4,3,2,1,0:T(8,128)S(1)} %fusion.47, f32[1,2,16,32,128]{4,3,2,1,0:T(8,128)S(1)} %bitcast.82, f32[1,2,16,32,128]{4,3,2,1,0:T(8,128)S(1)} %bitcast.81, ...), kind=kLoop, calls=%fused_computation.153 | loop fusion | flops 6291456 | bytes 16252928 | tf_op jit(solution)/shard_map/add | solution.py:160
  172.7 2.4 collective-permute-start.9
  175.1 3.2 %collective-permute-start.8 = (f32[2,2,3,32,128]{4,3,2,1,0:T(8,128)S(1)}, f32[2,2,3,32,128]{4,3,2,1,0:T(8,128)S(1)}, u32[]{:S(2)}, u32[]{:S(2)}) collective-permute-start(f32[2,2,3,32,128]{4,3,2,1,0:T(8,128)S(1)} %get-tuple-element.28), channel_id=1, source_target_pairs={{0,64},{64,128},{128,192},{1,65},{65,129},{129,193},{2,66},{66,130... | collective-permute-start | bytes 589832 | tf_op jit(solution)/shard_map/ppermute | solution.py:21
  178.3 2.5 fusion.1
  181.0 1.3 collective-permute-start.11
  182.3 5.6 %collective-permute-start.10 = (f32[2,2,22,3,128]{4,3,2,1,0:T(4,128)S(1)}, f32[2,2,22,3,128]{4,3,2,1,0:T(4,128)S(1)}, u32[]{:S(2)}, u32[]{:S(2)}) collective-permute-start(f32[2,2,22,3,128]{4,3,2,1,0:T(4,128)S(1)} %get-tuple-element.18), channel_id=1, source_target_pairs={{0,8},{8,16},{16,24},{24,32},{32,40},{40,48},{48,56},{1,9},{9,17},... | collective-permute-start | bytes 405512 | tf_op jit(solution)/shard_map/ppermute | solution.py:21
  188.5 1.9 collective-permute-done.11
  190.3 2.4 collective-permute-done.10
  193.1 1.7 fusion.12
  194.8 0.6 fusion.32
  195.4 1.3 fusion.70
  197.1 2.3 collective-permute-start.13
  199.4 3.5 %collective-permute-start.12 = (f32[2,2,3,32,128]{4,3,2,1,0:T(8,128)S(1)}, f32[2,2,3,32,128]{4,3,2,1,0:T(8,128)S(1)}, u32[]{:S(2)}, u32[]{:S(2)}) collective-permute-start(f32[2,2,3,32,128]{4,3,2,1,0:T(8,128)S(1)} %get-tuple-element.24), channel_id=1, source_target_pairs={{0,64},{64,128},{128,192},{1,65},{65,129},{129,193},{2,66},{66,130... | collective-permute-start | bytes 589832 | tf_op jit(solution)/shard_map/ppermute | solution.py:21
  202.9 2.5 fusion
  205.5 1.3 collective-permute-start.15
  206.8 6.3 %collective-permute-start.14 = (f32[2,2,22,3,128]{4,3,2,1,0:T(4,128)S(1)}, f32[2,2,22,3,128]{4,3,2,1,0:T(4,128)S(1)}, u32[]{:S(2)}, u32[]{:S(2)}) collective-permute-start(f32[2,2,22,3,128]{4,3,2,1,0:T(4,128)S(1)} %get-tuple-element.16), channel_id=1, source_target_pairs={{0,8},{8,16},{16,24},{24,32},{32,40},{40,48},{48,56},{1,9},{9,17},... | collective-permute-start | bytes 405512 | tf_op jit(solution)/shard_map/ppermute | solution.py:21
  213.6 1.6 collective-permute-done.15
  215.2 4.6 %collective-permute-done.14 = f32[2,2,22,3,128]{4,3,2,1,0:T(4,128)S(1)} collective-permute-done((f32[2,2,22,3,128]{4,3,2,1,0:T(4,128)S(1)}, f32[2,2,22,3,128]{4,3,2,1,0:T(4,128)S(1)}, u32[]{:S(2)}, u32[]{:S(2)}) %collective-permute-start.14) | collective-permute-done | bytes 135200 | tf_op jit(solution)/shard_map/ppermute | solution.py:21
  220.1 1.7 fusion.18
  221.8 0.6 fusion.27
  222.4 1.3 fusion.56
  224.1 0.9 copy-done.9
  225.0 1.6 multiply_reduce_fusion
  226.5 19.1 %psum.22 = f32[2]{0:T(128)S(1)} all-reduce(f32[2]{0:T(128)S(1)} %get-tuple-element.11), channel_id=1, replica_groups=mesh['px'=4,'py'=8,'dom'=8] {'py'}, use_global_device_ids=true, to_apply=%region_4.5 | all-reduce | flops 2 | bytes 16 | tf_op jit(solution)/shard_map/psum | solution.py:183
  245.7 9.2 %psum.23 = f32[2]{0:T(128)S(1)} all-reduce(f32[2]{0:T(128)S(1)} %psum.22), channel_id=1, replica_groups=mesh['px'=4,'py'=8,'dom'=8] {'px'}, use_global_device_ids=true, to_apply=%region_5.6 | all-reduce | flops 2 | bytes 16 | tf_op jit(solution)/shard_map/psum | solution.py:183
  255.5 19.2 %all_to_all.64 = f32[2,8,8192]{2,0,1:T(2,128)S(1)} all-to-all(f32[2,8,8192]{2,0,1:T(2,128)S(1)} %copy.55), channel_id=1, replica_groups=mesh['px'=4,'py'=8,'dom'=8] {'dom'}, dimensions={1} | all-to-all | bytes 1048576 | tf_op jit(solution)/shard_map/all_to_all | solution.py:187
  275.6 1.2 copy.57
  276.8 3.5 %all-to-all-start.2 = ((f32[8,2,8192]{2,1,0:T(2,128)}), f32[8,2,8192]{2,1,0:T(2,128)S(1)}, u32[]{:S(2)}, u32[]{:S(2)}) async-start(f32[8,2,8192]{2,1,0:T(2,128)} %copy.57), calls=%async_computation.2 | async-start | bytes 1048576 | tf_op jit(solution)/shard_map/all_to_all | solution.py:202
  280.3 0.8 slice_bitcast_fusion.2
  281.1 15.1 %all-to-all-done.2 = f32[8,2,8192]{2,1,0:T(2,128)S(1)} async-done(((f32[8,2,8192]{2,1,0:T(2,128)}), f32[8,2,8192]{2,1,0:T(2,128)S(1)}, u32[]{:S(2)}, u32[]{:S(2)}) %all-to-all-start.2) | async-done | bytes 524320 | tf_op jit(solution)/shard_map/all_to_all | solution.py:202
  296.5 0.9 reshape.285
  (100 shorter events, 7.8 us)
Async XLA Ops:
  0.6 8.9 %copy-start.11 = (f32[16,32,128]{2,1,0:T(8,128)S(1)}, f32[16,32,128]{2,1,0:T(8,128)}, u32[]{:S(2)}) copy-start(f32[16,32,128]{2,1,0:T(8,128)} %param.12) | copy-start | bytes 786436
  0.6 13.2 %copy-start.8 = (f32[2,16,32,128]{3,2,1,0:T(8,128)S(1)}, f32[2,16,32,128]{3,2,1,0:T(8,128)}, u32[]{:S(2)}) copy-start(f32[2,16,32,128]{3,2,1,0:T(8,128)} %param.11) | copy-start | bytes 1572868
  2.5 37.5 %collective-permute-start.3 = (f32[2,2,3,32,128]{4,3,2,1,0:T(8,128)}, f32[2,2,3,32,128]{4,3,2,1,0:T(8,128)S(1)}, u32[]{:S(2)}, u32[]{:S(2)}) collective-permute-start(f32[2,2,3,32,128]{4,3,2,1,0:T(8,128)} %get-tuple-element.33), channel_id=1, source_target_pairs={{64,0},{128,64},{192,128},{65,1},{129,65},{193,129},{66,2},{130,66... | collective-permute-start | bytes 589832 | tf_op jit(solution)/shard_map/ppermute | solution.py:23
  7.6 32.4 %collective-permute-start.2 = (f32[2,2,3,32,128]{4,3,2,1,0:T(8,128)S(1)}, f32[2,2,3,32,128]{4,3,2,1,0:T(8,128)S(1)}, u32[]{:S(2)}, u32[]{:S(2)}) collective-permute-start(f32[2,2,3,32,128]{4,3,2,1,0:T(8,128)S(1)} %get-tuple-element.32), channel_id=1, source_target_pairs={{0,64},{64,128},{128,192},{1,65},{65,129},{129,193},{2,66},{66,130... | collective-permute-start | bytes 589832 | tf_op jit(solution)/shard_map/ppermute | solution.py:21
  9.5 22.0 %collective-permute-start = (f32[3,32,128]{2,1,0:T(8,128)S(1)}, f32[3,32,128]{2,1,0:T(8,128)S(1)}, u32[]{:S(2)}, u32[]{:S(2)}) collective-permute-start(f32[3,32,128]{2,1,0:T(8,128)S(1)} %get-tuple-element.39), channel_id=1, source_target_pairs={{0,64},{64,128},{128,192},{1,65},{65,129},{129,193},{2,66},{66,130... | collective-permute-start | bytes 147464 | tf_op jit(solution)/shard_map/ppermute | solution.py:21
  11.5 20.1 %collective-permute-start.1 = (f32[3,32,128]{2,1,0:T(8,128)S(1)}, f32[3,32,128]{2,1,0:T(8,128)S(1)}, u32[]{:S(2)}, u32[]{:S(2)}) collective-permute-start(f32[3,32,128]{2,1,0:T(8,128)S(1)} %get-tuple-element.38), channel_id=1, source_target_pairs={{64,0},{128,64},{192,128},{65,1},{129,65},{193,129},{66,2},{130,66... | collective-permute-start | bytes 147464 | tf_op jit(solution)/shard_map/ppermute | solution.py:23
  14.0 8.9 %copy-start.16 = (f32[2,3]{1,0:T(2,128)S(1)}, f32[2,3]{1,0:T(2,128)}, u32[]{:S(2)}) copy-start(f32[2,3]{1,0:T(2,128)} %param.18) | copy-start | bytes 76
  14.0 9.2 %copy-start.18 = (s32[2]{0:T(128)S(1)}, s32[2]{0:T(128)}, u32[]{:S(2)}) copy-start(s32[2]{0:T(128)} %param.17) | copy-start | bytes 28
  14.0 9.3 %copy-start.17 = (s32[2,1024]{1,0:T(2,128)S(1)}, s32[2,1024]{1,0:T(2,128)}, u32[]{:S(2)}) copy-start(s32[2,1024]{1,0:T(2,128)} %param.19) | copy-start | bytes 24580
  14.0 9.3 %copy-start.14 = (f32[2,3,1024]{2,0,1:T(2,128)S(1)}, f32[2,3,1024]{2,0,1:T(2,128)}, u32[]{:S(2)}) copy-start(f32[2,3,1024]{2,0,1:T(2,128)} %param.20) | copy-start | bytes 73732
  14.0 9.3 %copy-start.15 = (s32[6]{0:T(128)S(1)}, s32[6]{0:T(128)}, u32[]{:S(2)}) copy-start(s32[6]{0:T(128)} %param.21) | copy-start | bytes 76
  15.3 35.4 %all-to-all-start = ((f32[2,8,8192]{2,0,1:T(2,128)}), f32[2,8,8192]{2,0,1:T(2,128)S(1)}, u32[]{:S(2)}, u32[]{:S(2)}) async-start(f32[2,8,8192]{2,0,1:T(2,128)} %copy.54), calls=%async_computation | async-start | bytes 1048576 | tf_op jit(solution)/shard_map/all_to_all | solution.py:186
  31.6 7.6 %collective-permute-start.5 = (f32[22,3,128]{2,1,0:T(4,128)S(1)}, f32[22,3,128]{2,1,0:T(4,128)S(1)}, u32[]{:S(2)}, u32[]{:S(2)}) collective-permute-start(f32[22,3,128]{2,1,0:T(4,128)S(1)} %get-tuple-element.37), channel_id=1, source_target_pairs={{8,0},{16,8},{24,16},{32,24},{40,32},{48,40},{56,48},{9,1},{17,9},... | collective-permute-start | bytes 101384 | tf_op jit(solution)/shard_map/ppermute | solution.py:23
  32.9 6.6 %collective-permute-start.4 = (f32[22,3,128]{2,1,0:T(4,128)S(1)}, f32[22,3,128]{2,1,0:T(4,128)S(1)}, u32[]{:S(2)}, u32[]{:S(2)}) collective-permute-start(f32[22,3,128]{2,1,0:T(4,128)S(1)} %get-tuple-element.36), channel_id=1, source_target_pairs={{0,8},{8,16},{16,24},{24,32},{32,40},{40,48},{48,56},{1,9},{9,17},... | collective-permute-start | bytes 101384 | tf_op jit(solution)/shard_map/ppermute | solution.py:21
  39.1 1.0 copy-start
  39.1 1.2 copy-start.1
  40.0 10.6 %copy-start.4 = (f32[2,2,3,32,128]{4,3,2,1,0:T(8,128)}, f32[2,2,3,32,128]{4,3,2,1,0:T(8,128)S(1)}, u32[]{:S(2)}) copy-start(f32[2,2,3,32,128]{4,3,2,1,0:T(8,128)S(1)} %collective-permute-done.3) | copy-start | bytes 589828
  40.3 10.3 %copy-start.6 = (f32[2,2,3,32,128]{4,3,2,1,0:T(8,128)}, f32[2,2,3,32,128]{4,3,2,1,0:T(8,128)S(1)}, u32[]{:S(2)}) copy-start(f32[2,2,3,32,128]{4,3,2,1,0:T(8,128)S(1)} %collective-permute-done.2) | copy-start | bytes 589828
  41.2 104.7 %collective-permute-start.7 = (f32[2,2,22,3,128]{4,3,2,1,0:T(4,128)}, f32[2,2,22,3,128]{4,3,2,1,0:T(4,128)}, u32[]{:S(2)}, u32[]{:S(2)}) collective-permute-start(f32[2,2,22,3,128]{4,3,2,1,0:T(4,128)} %get-tuple-element.21), channel_id=1, source_target_pairs={{8,0},{16,8},{24,16},{32,24},{40,32},{48,40},{56,48},{9,1},{17,9},... | collective-permute-start | bytes 405512 | tf_op jit(solution)/shard_map/ppermute | solution.py:23
  42.5 103.4 %collective-permute-start.6 = (f32[2,2,22,3,128]{4,3,2,1,0:T(4,128)}, f32[2,2,22,3,128]{4,3,2,1,0:T(4,128)}, u32[]{:S(2)}, u32[]{:S(2)}) collective-permute-start(f32[2,2,22,3,128]{4,3,2,1,0:T(4,128)} %get-tuple-element.20), channel_id=1, source_target_pairs={{0,8},{8,16},{16,24},{24,32},{32,40},{40,48},{48,56},{1,9},{9,17},... | collective-permute-start | bytes 405512 | tf_op jit(solution)/shard_map/ppermute | solution.py:21
  138.0 23.5 %all-to-all-start.3 = ((f32[8,2,8192]{2,1,0:T(2,128)}), f32[8,2,8192]{2,1,0:T(2,128)}, u32[]{:S(2)}, u32[]{:S(2)}) async-start(f32[8,2,8192]{2,1,0:T(2,128)} %copy.60), calls=%async_computation.3 | async-start | bytes 1048576 | tf_op jit(solution)/shard_map/all_to_all | solution.py:203
  143.5 2.4 copy-start.5
  143.5 2.5 copy-start.7
  165.6 2.4 copy-start.2
  165.6 2.4 copy-start.10
  165.6 2.4 copy-start.12
  168.0 4.3 %copy-start.13 = (f32[2,512,128]{2,1,0:T(8,128)S(1)}, f32[2,512,128]{2,1,0:T(8,128)}, u32[]{:S(2)}) copy-start(f32[2,512,128]{2,1,0:T(8,128)} %fusion.2) | copy-start | bytes 1572868
  172.7 8.1 %collective-permute-start.9 = (f32[2,2,3,32,128]{4,3,2,1,0:T(8,128)S(1)}, f32[2,2,3,32,128]{4,3,2,1,0:T(8,128)S(1)}, u32[]{:S(2)}, u32[]{:S(2)}) collective-permute-start(f32[2,2,3,32,128]{4,3,2,1,0:T(8,128)S(1)} %get-tuple-element.29), channel_id=1, source_target_pairs={{64,0},{128,64},{192,128},{65,1},{129,65},{193,129},{66,2},{130,66... | collective-permute-start | bytes 589832 | tf_op jit(solution)/shard_map/ppermute | solution.py:23
  175.1 5.8 %collective-permute-start.8 = (f32[2,2,3,32,128]{4,3,2,1,0:T(8,128)S(1)}, f32[2,2,3,32,128]{4,3,2,1,0:T(8,128)S(1)}, u32[]{:S(2)}, u32[]{:S(2)}) collective-permute-start(f32[2,2,3,32,128]{4,3,2,1,0:T(8,128)S(1)} %get-tuple-element.28), channel_id=1, source_target_pairs={{0,64},{64,128},{128,192},{1,65},{65,129},{129,193},{2,66},{66,130... | collective-permute-start | bytes 589832 | tf_op jit(solution)/shard_map/ppermute | solution.py:21
  181.0 9.3 %collective-permute-start.11 = (f32[2,2,22,3,128]{4,3,2,1,0:T(4,128)S(1)}, f32[2,2,22,3,128]{4,3,2,1,0:T(4,128)S(1)}, u32[]{:S(2)}, u32[]{:S(2)}) collective-permute-start(f32[2,2,22,3,128]{4,3,2,1,0:T(4,128)S(1)} %get-tuple-element.19), channel_id=1, source_target_pairs={{8,0},{16,8},{24,16},{32,24},{40,32},{48,40},{56,48},{9,1},{17,9},... | collective-permute-start | bytes 405512 | tf_op jit(solution)/shard_map/ppermute | solution.py:23
  182.3 5.8 %copy-start.3 = (f32[19,32,128]{2,1,0:T(8,128)S(1)}, f32[19,32,128]{2,1,0:T(8,128)}, u32[]{:S(2)}) copy-start(f32[19,32,128]{2,1,0:T(8,128)} %fusion.116) | copy-start | bytes 933892
  182.3 10.5 %collective-permute-start.10 = (f32[2,2,22,3,128]{4,3,2,1,0:T(4,128)S(1)}, f32[2,2,22,3,128]{4,3,2,1,0:T(4,128)S(1)}, u32[]{:S(2)}, u32[]{:S(2)}) collective-permute-start(f32[2,2,22,3,128]{4,3,2,1,0:T(4,128)S(1)} %get-tuple-element.18), channel_id=1, source_target_pairs={{0,8},{8,16},{16,24},{24,32},{32,40},{40,48},{48,56},{1,9},{9,17},... | collective-permute-start | bytes 405512 | tf_op jit(solution)/shard_map/ppermute | solution.py:21
  197.1 8.3 %collective-permute-start.13 = (f32[2,2,3,32,128]{4,3,2,1,0:T(8,128)S(1)}, f32[2,2,3,32,128]{4,3,2,1,0:T(8,128)S(1)}, u32[]{:S(2)}, u32[]{:S(2)}) collective-permute-start(f32[2,2,3,32,128]{4,3,2,1,0:T(8,128)S(1)} %get-tuple-element.25), channel_id=1, source_target_pairs={{64,0},{128,64},{192,128},{65,1},{129,65},{193,129},{66,2},{130,66... | collective-permute-start | bytes 589832 | tf_op jit(solution)/shard_map/ppermute | solution.py:23
  199.4 6.0 %collective-permute-start.12 = (f32[2,2,3,32,128]{4,3,2,1,0:T(8,128)S(1)}, f32[2,2,3,32,128]{4,3,2,1,0:T(8,128)S(1)}, u32[]{:S(2)}, u32[]{:S(2)}) collective-permute-start(f32[2,2,3,32,128]{4,3,2,1,0:T(8,128)S(1)} %get-tuple-element.24), channel_id=1, source_target_pairs={{0,64},{64,128},{128,192},{1,65},{65,129},{129,193},{2,66},{66,130... | collective-permute-start | bytes 589832 | tf_op jit(solution)/shard_map/ppermute | solution.py:21
  205.5 9.8 %collective-permute-start.15 = (f32[2,2,22,3,128]{4,3,2,1,0:T(4,128)S(1)}, f32[2,2,22,3,128]{4,3,2,1,0:T(4,128)S(1)}, u32[]{:S(2)}, u32[]{:S(2)}) collective-permute-start(f32[2,2,22,3,128]{4,3,2,1,0:T(4,128)S(1)} %get-tuple-element.17), channel_id=1, source_target_pairs={{8,0},{16,8},{24,16},{32,24},{40,32},{48,40},{56,48},{9,1},{17,9},... | collective-permute-start | bytes 405512 | tf_op jit(solution)/shard_map/ppermute | solution.py:23
  206.8 13.1 %collective-permute-start.14 = (f32[2,2,22,3,128]{4,3,2,1,0:T(4,128)S(1)}, f32[2,2,22,3,128]{4,3,2,1,0:T(4,128)S(1)}, u32[]{:S(2)}, u32[]{:S(2)}) collective-permute-start(f32[2,2,22,3,128]{4,3,2,1,0:T(4,128)S(1)} %get-tuple-element.16), channel_id=1, source_target_pairs={{0,8},{8,16},{16,24},{24,32},{32,40},{40,48},{48,56},{1,9},{9,17},... | collective-permute-start | bytes 405512 | tf_op jit(solution)/shard_map/ppermute | solution.py:21
  223.9 1.0 copy-start.9
  276.8 19.5 %all-to-all-start.2 = ((f32[8,2,8192]{2,1,0:T(2,128)}), f32[8,2,8192]{2,1,0:T(2,128)S(1)}, u32[]{:S(2)}, u32[]{:S(2)}) async-start(f32[8,2,8192]{2,1,0:T(2,128)} %copy.57), calls=%async_computation.2 | async-start | bytes 1048576 | tf_op jit(solution)/shard_map/all_to_all | solution.py:202
